TPU v7x, 32 devices: a whole 2x2x4 slice. The times are simulated.
32 devices in a mesh: dp: 4 (over y, x), seq: 4 (over z), tensor: 2 (over core).
Axes of the slice: x: 2, y: 2, z: 4, core: 2. Of those that a mesh axis runs over, the one named last changes fastest.
Arguments:
- queries: bfloat16 [4, 256, 8192], P('dp', 'seq', 'tensor'), may hold values from -6 to 6
- new_keys: bfloat16 [4, 256, 1024], P('dp', 'seq', 'tensor'), may hold values from -6 to 6
- new_values: bfloat16 [4, 256, 1024], P('dp', 'seq', 'tensor'), may hold values from -6 to 6
- cache_keys: bfloat16 [4, 2048, 1024], P('dp', 'seq', 'tensor'), may hold values from -6 to 6
- cache_values: bfloat16 [4, 2048, 1024], P('dp', 'seq', 'tensor'), may hold values from -6 to 6
- keep_lengths: int32 [4, 4], P('dp', 'seq'), may hold values from 1 to 512
- cache_doc: int32 [4, 2048], P('dp', 'seq'), may hold values from 0 to 1
- new_doc: int32 [4, 256], P('dp', 'seq'), may hold values from 0 to 1, never falling along the last dimension, each value on 1 to 160 neighbouring positions
- out_weight: bfloat16 [8192, 8192], P('tensor', 'dp'), may hold values from -0.0625 to 0.0625
Outputs:
- mixed_out: bfloat16 [4, 256, 4, 2048], P('dp', 'seq', None, 'tensor')
Inputs may be any that keep to these rules, and one draw needn't show every extreme that they name: `keep_lengths`: valid cache rows of a shard come first. `cache_doc`: documents 0 and 1 of the pack. `new_doc`: never falling along the tokens of a pack; both documents present.
All inputs are finite; a program needn't handle non-finite values.
Results may differ from a plain program's by a relative error of at most 0.0056.
Values may be sent and summed in bfloat16 or wider, within the bound.
A program may use at most 128 MiB of HBM per device.

v0:
```python
import math

import jax
import jax.numpy as jnp
from jax import lax
from jax.sharding import PartitionSpec as P

HD = 128


masked_score = -1e30


def softmax_terms(scores, visible, value_rows):
    scores = jnp.where(visible, scores, masked_score)
    top_score = jnp.max(scores, axis=-1)
    weights = jnp.where(visible, jnp.exp(scores - top_score[..., None]), 0.0)
    weight_sum = jnp.sum(weights, axis=-1)
    summed = jnp.dot(weights.astype(jnp.bfloat16), value_rows, preferred_element_type=jnp.float32)
    return (top_score, weight_sum, summed)


def masked_terms(query_rows, row_doc, key_rows, value_rows, doc_rows, length, score_scale):
    scores = jnp.dot(query_rows, key_rows.T, preferred_element_type=jnp.float32) * score_scale
    positions = jnp.arange(key_rows.shape[0], dtype=jnp.int32)
    visible = (positions[None, :] < length) & (doc_rows[None, :] == row_doc[:, None])
    return softmax_terms(scores, visible, value_rows)


def join_terms(earlier, later):
    top_score = jnp.maximum(earlier[0], later[0])
    early_factor = jnp.exp(earlier[0] - top_score)
    late_factor = jnp.exp(later[0] - top_score)
    weight_sum = earlier[1] * early_factor + later[1] * late_factor
    summed = earlier[2] * early_factor[..., None] + later[2] * late_factor[..., None]
    return (top_score, weight_sum, summed)


def local(
    queries,
    new_keys,
    new_values,
    cache_keys,
    cache_values,
    keep_lengths,
    cache_doc,
    new_doc,
    out_weight,
):
    score_scale = HD ** (-0.5)
    tok_rows = queries.shape[1]
    local_heads = queries.shape[2] // HD
    local_kv = cache_keys.shape[2] // HD
    head_group = local_heads // local_kv
    cache_rows = cache_keys.shape[1]
    all_queries, all_keys, all_values, all_doc = (
        lax.all_gather(queries, "seq", axis=1, tiled=True),
        lax.all_gather(new_keys, "seq", axis=1, tiled=True),
        lax.all_gather(new_values, "seq", axis=1, tiled=True),
        lax.all_gather(new_doc, "seq", axis=1, tiled=True),
    )
    pack_len = all_queries.shape[1]
    query_rows = all_queries[0].reshape(pack_len, local_kv, head_group, HD).transpose(1, 0, 2, 3)
    row_doc = jnp.repeat(all_doc[0], head_group)
    block_size = math.gcd(pack_len * head_group, 1024)
    block_count = pack_len * head_group // block_size
    query_blocks = query_rows.reshape(local_kv * block_count, block_size, HD)
    doc_blocks = jnp.tile(row_doc.reshape(block_count, block_size), (local_kv, 1))
    head_ids = jnp.repeat(jnp.arange(local_kv, dtype=jnp.int32), block_count)
    key_heads = cache_keys[0].reshape(cache_rows, local_kv, HD).transpose(1, 0, 2)
    value_heads = cache_values[0].reshape(cache_rows, local_kv, HD).transpose(1, 0, 2)
    doc_rows = cache_doc[0]
    length = keep_lengths[0, 0]

    def block_terms(inputs):
        query_block, block_doc, head_index = inputs
        key_rows = lax.dynamic_index_in_dim(key_heads, head_index, 0, keepdims=False)
        value_rows = lax.dynamic_index_in_dim(value_heads, head_index, 0, keepdims=False)
        return masked_terms(
            query_block, block_doc, key_rows, value_rows, doc_rows, length, score_scale
        )

    block_tops, block_sums, block_partial = lax.map(
        block_terms, (query_blocks, doc_blocks, head_ids)
    )
    cache_top = block_tops.reshape(local_kv, pack_len, head_group)
    cache_sum = block_sums.reshape(local_kv, pack_len, head_group)
    cache_partial = block_partial.reshape(local_kv, pack_len, head_group, HD)
    my_start = lax.axis_index("seq") * tok_rows
    shares = (
        lax.all_to_all(cache_top[None], "seq", split_axis=2, concat_axis=0, tiled=True),
        lax.all_to_all(cache_sum[None], "seq", split_axis=2, concat_axis=0, tiled=True),
        lax.all_to_all(cache_partial[None], "seq", split_axis=2, concat_axis=0, tiled=True),
    )
    overall_top = jnp.max(shares[0], axis=0)
    factors = jnp.exp(shares[0] - overall_top[None])
    merged = (
        overall_top,
        jnp.sum(shares[1] * factors, 0),
        jnp.sum(shares[2] * factors[..., None], 0),
    )
    own_queries = (
        queries[0]
        .reshape(tok_rows, local_kv, head_group, HD)
        .transpose(1, 0, 2, 3)
        .reshape(local_kv, tok_rows * head_group, HD)
    )
    fresh_keys = all_keys[0].reshape(pack_len, local_kv, HD).transpose(1, 0, 2)
    fresh_values = all_values[0].reshape(pack_len, local_kv, HD).transpose(1, 0, 2)
    scores = (
        jnp.einsum("gqd,gkd->gqk", own_queries, fresh_keys, preferred_element_type=jnp.float32)
        * score_scale
    )
    row_token = my_start + jnp.arange(tok_rows * head_group, dtype=jnp.int32) // head_group
    own_doc = jnp.repeat(new_doc[0], head_group)
    key_index = jnp.arange(pack_len, dtype=jnp.int32)
    visible = (
        (key_index[None, :] <= row_token[:, None]) & (all_doc[0][None, :] == own_doc[:, None])
    )[None]
    scores = jnp.where(visible, scores, masked_score)
    fresh_top = jnp.max(scores, axis=-1)
    weights = jnp.where(visible, jnp.exp(scores - fresh_top[..., None]), 0.0)
    fresh_sum = jnp.sum(weights, axis=-1)
    fresh_partial = jnp.einsum(
        "gqk,gkd->gqd",
        weights.astype(jnp.bfloat16),
        fresh_values,
        preferred_element_type=jnp.float32,
    )
    fresh = (
        fresh_top.reshape(local_kv, tok_rows, head_group),
        fresh_sum.reshape(local_kv, tok_rows, head_group),
        fresh_partial.reshape(local_kv, tok_rows, head_group, HD),
    )
    final = join_terms(merged, fresh)
    attended = (
        (final[2] / final[1][..., None])
        .transpose(1, 0, 2, 3)
        .reshape(1, tok_rows, local_heads * HD)
        .astype(jnp.bfloat16)
    )
    partial_cols = jnp.einsum(
        "ptf,fc->ptc",
        lax.all_gather(attended, "dp", axis=0, tiled=True),
        out_weight,
        preferred_element_type=jnp.float32,
    )
    summed_cols = lax.psum_scatter(partial_cols, "tensor", scatter_dimension=2, tiled=True).astype(
        jnp.bfloat16
    )
    return lax.all_to_all(summed_cols[:, :, None, :], "dp", split_axis=0, concat_axis=2, tiled=True)


def solution(mesh):
    placed = (
        P("dp", "seq", "tensor"),
        P("dp", "seq", "tensor"),
        P("dp", "seq", "tensor"),
        P("dp", "seq", "tensor"),
        P("dp", "seq", "tensor"),
        P("dp", "seq"),
        P("dp", "seq"),
        P("dp", "seq"),
        P("tensor", "dp"),
    )
    return jax.shard_map(
        local, mesh=mesh, in_specs=placed, out_specs=P("dp", "seq", None, "tensor"), check_vma=False
    )
```

profile of v0, /device:TPU:25, one launch (start us, length us, event | category | flops | bytes accessed | tf_op | source)
XLA Modules:
  0.0 351.4 jit_solution(5409728483405460496)
XLA Ops:
  10.0 4.2 %all-reduce = s32[256]{0:T(256)S(1)} all-reduce(s32[256]{0:T(256)S(1)} %bitcast_dynamic-update-slice_fusion), channel_id=1, replica_groups=mesh['dp'=4,'seq'=4,'tensor'=2] {'seq'}, use_global_device_ids=true, to_apply=%add | all-reduce | flops 256 | bytes 2048
  16.0 37.8 %all-gather.3.cloned.1.call-done = bf16[1,256,4096]{2,1,0:T(8,128)(2,1)} async-done(((bf16[1,64,4096]{2,1,0:T(8,128)(2,1)}), bf16[1,256,4096]{2,1,0:T(8,128)(2,1)}) %all-gather.3.cloned.1.call-update) | async-done | bytes 2097168 | tf_op jit(solution)/shard_map/all_gather | solution.py:57
  53.8 2.1 copy.112
  55.9 1.7 copy.83
  57.6 59.2 %while.14 = (s32[]{:T(128)}, f32[8,1024]{1,0:T(8,128)S(1)}, f32[8,1024]{1,0:T(8,128)S(1)}, f32[8,1024,128]{2,1,0:T(8,128)}, s32[]{:T(128)}, /*index=5*/s32[1,512...) while((s32[]{:T(128)}, f32[8,1024]{1,0:T(8,128)S(1)}, ...), condition=%wide.region_3.4_spmd, body=%wide.region_0.3_spmd.sunk | while | flops 276298240 | bytes 7401691 | solution.py:83
  70.7 1.7 fusion.60
  78.1 1.7 fusion.60
  83.0 1.6 fusion.58
  85.5 1.7 fusion.60
  92.9 1.7 fusion.60
  100.3 1.7 fusion.60
  112.6 1.6 fusion.58
  115.1 1.7 fusion.60
  118.6 5.1 %all-to-all-start.1 = ((f32[4,1,2048]{2,1,0:T(1,128)}), f32[4,1,2048]{2,1,0:T(1,128)S(1)}, u32[]{:S(2)}, u32[]{:S(2)}) async-start(f32[4,1,2048]{2,1,0:T(1,128)} %reshape.172), calls=%async_computation.1 | async-start | bytes 65536 | tf_op jit(solution)/shard_map/all_to_all | solution.py:91
  125.5 5.9 %all-to-all-start.2 = ((f32[4,1,2048]{2,1,0:T(1,128)}), f32[4,1,2048]{2,1,0:T(1,128)S(1)}, u32[]{:S(2)}, u32[]{:S(2)}) async-start(f32[4,1,2048]{2,1,0:T(1,128)} %reshape.174), calls=%async_computation.2 | async-start | bytes 65536 | tf_op jit(solution)/shard_map/all_to_all | solution.py:92
  131.4 4.7 %copy.88 = f32[1,4,256,8,128]{4,3,1,0,2:T(8,128)} copy(f32[1,4,256,8,128]{4,3,2,1,0:T(8,128)} %bitcast.127) | data formatting | bytes 8388608 | tf_op jit(solution)/shard_map/broadcast_in_dim;reshape | solution.py:93
  136.7 4.8 %all-to-all-start = ((f32[1,4,256,8,128]{4,3,1,0,2:T(8,128)}), f32[1,4,256,8,128]{4,3,1,0,2:T(8,128)}, u32[]{:S(2)}, u32[]{:S(2)}) async-start(f32[1,4,256,8,128]{4,3,1,0,2:T(8,128)} %copy.88), calls=%async_computation | async-start | bytes 8388608 | tf_op jit(solution)/shard_map/all_to_all | solution.py:93
  141.8 97.3 %all_gather.20 = bf16[1,256,512]{2,1,0:T(8,128)(2,1)S(1)} all-gather(bf16[1,64,512]{2,1,0:T(8,128)(2,1)S(1)} %copy-done.4), channel_id=1, replica_groups=mesh['dp'=4,'seq'=4,'tensor'=2] {'seq'}, dimensions={1}, use_global_device_ids=true | all-gather | bytes 327680 | tf_op jit(solution)/shard_map/all_gather | solution.py:58
  240.1 11.7 %all_gather.21 = bf16[1,256,512]{2,1,0:T(8,128)(2,1)S(1)} all-gather(bf16[1,64,512]{2,1,0:T(8,128)(2,1)S(1)} %copy-done.5), channel_id=1, replica_groups=mesh['dp'=4,'seq'=4,'tensor'=2] {'seq'}, dimensions={1}, use_global_device_ids=true | all-gather | bytes 327680 | tf_op jit(solution)/shard_map/all_gather | solution.py:59
  262.6 2.9 multiply_reduce_fusion
  267.6 41.3 %all-gather.5.cloned.1.call-done = bf16[4,64,4096]{2,1,0:T(8,128)(2,1)} async-done(((bf16[1,64,4096]{2,1,0:T(8,128)(2,1)}), bf16[4,64,4096]{2,1,0:T(8,128)(2,1)}) %all-gather.5.cloned.1.call-update) | async-done | bytes 2097168 | tf_op jit(solution)/shard_map/all_gather | solution.py:144
  308.9 12.2 %fusion.17 = f32[4,64,2048]{2,1,0:T(8,128)} fusion(bf16[4,64,4096]{2,1,0:T(8,128)(2,1)} %all-gather.5.cloned.1.call-done, bf16[4096,2048]{1,0:T(8,128)(2,1)} %param.19), kind=kOutput, calls=%fused_computation.22 | convolution fusion | flops 4294967296 | bytes 20971520 | tf_op jit(solution)/shard_map/ptf,fc->ptc/dot_general | solution.py:142
  321.2 10.6 %reduce-scatter.2.cloned.1.call-done = f32[4,64,1024]{2,1,0:T(8,128)} async-done(((f32[4,64,2048]{2,1,0:T(8,128)}), f32[4,64,1024]{2,1,0:T(8,128)}) %reduce-scatter.2.cloned.1.call-update) | async-done | bytes 1048592 | tf_op jit(solution)/shard_map/reduce_scatter | solution.py:148
  333.1 10.6 %all_to_all.72 = bf16[4,64,1,1024]{3,1,2,0:T(8,128)(2,1)S(1)} all-to-all(bf16[4,64,1,1024]{3,1,2,0:T(8,128)(2,1)S(1)} %convert_bitcast_fusion), channel_id=1, replica_groups=mesh['dp'=4,'seq'=4,'tensor'=2] {'dp'}, dimensions={0} | all-to-all | bytes 1048576 | tf_op jit(solution)/shard_map/all_to_all | solution.py:151
  (138 shorter events, 55.1 us)
Async XLA Ops:
  6.5 9.2 %copy-start.1 = (bf16[1,512,512]{2,1,0:T(8,128)(2,1)S(1)}, bf16[1,512,512]{2,1,0:T(8,128)(2,1)}, u32[]{:S(2)}) copy-start(bf16[1,512,512]{2,1,0:T(8,128)(2,1)} %param.15) | copy-start | bytes 1572868
  6.5 47.3 %all-gather.3.cloned.1.call-start = ((), (), s32[]{:S(2)}) async-start(), calls=%async_computation.5 | async-start | bytes 2621440 | tf_op jit(solution)/shard_map/all_gather | solution.py:57
  55.9 1.7 copy-start.7
  118.6 6.9 %all-to-all-start.1 = ((f32[4,1,2048]{2,1,0:T(1,128)}), f32[4,1,2048]{2,1,0:T(1,128)S(1)}, u32[]{:S(2)}, u32[]{:S(2)}) async-start(f32[4,1,2048]{2,1,0:T(1,128)} %reshape.172), calls=%async_computation.1 | async-start | bytes 65536 | tf_op jit(solution)/shard_map/all_to_all | solution.py:91
  125.5 10.6 %copy-start.2 = (f32[4,1,2048]{2,1,0:T(1,128)}, f32[4,1,2048]{2,1,0:T(1,128)S(1)}, u32[]{:S(2)}) copy-start(f32[4,1,2048]{2,1,0:T(1,128)S(1)} %all-to-all-done.1) | copy-start | bytes 98308
  125.5 10.7 %all-to-all-start.2 = ((f32[4,1,2048]{2,1,0:T(1,128)}), f32[4,1,2048]{2,1,0:T(1,128)S(1)}, u32[]{:S(2)}, u32[]{:S(2)}) async-start(f32[4,1,2048]{2,1,0:T(1,128)} %reshape.174), calls=%async_computation.2 | async-start | bytes 65536 | tf_op jit(solution)/shard_map/all_to_all | solution.py:92
  136.1 5.5 %copy-start.9 = (s32[1,64]{1,0:T(1,128)S(1)}, s32[1,64]{1,0:T(1,128)}, u32[]{:S(2)}) copy-start(s32[1,64]{1,0:T(1,128)} %param.18) | copy-start | bytes 772
  136.1 5.7 %copy-start.4 = (bf16[1,64,512]{2,1,0:T(8,128)(2,1)S(1)}, bf16[1,64,512]{2,1,0:T(8,128)(2,1)}, u32[]{:S(2)}) copy-start(bf16[1,64,512]{2,1,0:T(8,128)(2,1)} %param.12) | copy-start | bytes 196612
  136.1 104.0 %copy-start.5 = (bf16[1,64,512]{2,1,0:T(8,128)(2,1)S(1)}, bf16[1,64,512]{2,1,0:T(8,128)(2,1)}, u32[]{:S(2)}) copy-start(bf16[1,64,512]{2,1,0:T(8,128)(2,1)} %param.13) | copy-start | bytes 196612
  136.1 0.6 copy-start.3
  136.7 125.8 %all-to-all-start = ((f32[1,4,256,8,128]{4,3,1,0,2:T(8,128)}), f32[1,4,256,8,128]{4,3,1,0,2:T(8,128)}, u32[]{:S(2)}, u32[]{:S(2)}) async-start(f32[1,4,256,8,128]{4,3,1,0,2:T(8,128)} %copy.88), calls=%async_computation | async-start | bytes 8388608 | tf_op jit(solution)/shard_map/all_to_all | solution.py:93
  141.6 110.6 %copy-start = (bf16[1,64,4096]{2,1,0:T(8,128)(2,1)S(1)}, bf16[1,64,4096]{2,1,0:T(8,128)(2,1)}, u32[]{:S(2)}) copy-start(bf16[1,64,4096]{2,1,0:T(8,128)(2,1)} %param.11) | copy-start | bytes 1572868
  141.6 167.3 %all-gather.5.cloned.1.call-start = ((), (), s32[]{:S(2)}) async-start(), calls=%async_computation.6 | async-start | bytes 2621440 | tf_op jit(solution)/shard_map/all_gather | solution.py:144
  253.9 0.9 copy-start.8
  257.0 5.2 %copy-start.6 = (f32[4,64,8]{1,2,0:T(8,128)S(1)}, f32[4,64,8]{1,2,0:T(8,128)}, u32[]{:S(2)}) copy-start(f32[4,64,8]{1,2,0:T(8,128)} %copy.105) | copy-start | bytes 24580
  267.5 64.3 %reduce-scatter.2.cloned.1.call-start = ((), (), s32[]{:S(2)}) async-start(), calls=%async_computation.7 | async-start | bytes 3145728 | tf_op jit(solution)/shard_map/reduce_scatter | solution.py:148
Sparse Core Ops, SparseCore 0:
  8.9 44.8 all-gather.2
  267.7 41.1 all-gather.4
  321.3 10.4 reduce-scatter.1
where the time goes:
time: 356 us; the launch traced here: 351 us
  blocking collectives  124 us (35%)
  waiting for transfers between devices  90.5 us (25%)
  matrix products  41.6 us (12%)
  local copies, waits for them, and re-layouts  30 us (8%)
  other arithmetic  19.6 us (6%)
  starting transfers between devices  15.9 us (4%)
  loops' own time  15.9 us (4%)
  between operations  14.2 us (4%)
    all_gather x1, blocking collectives, local(): lax.all_gather(new_keys, 'seq', axis=1, tiled=True)  97.3 us
    all_gather x1, waiting for transfers between devices, local(): lax.all_gather(attended, 'dp', axis=0, tiled=True)  41.3 us
    all_gather x1, waiting for transfers between devices, local(): lax.all_gather(queries, 'seq', axis=1, tiled=True)  37.8 us
    another operation x1, loops' own time, local(): lax.map(block_terms, (query_blocks, doc_blocks, head_ids))  15.9 us
    dot_general x8, matrix products, softmax_terms(): jnp.dot(weights.astype(jnp.bfloat16), value_rows, preferred_element_type=...  13.2 us
    dot_general x8, matrix products, masked_terms(): jnp.dot(query_rows, key_rows.T, preferred_element_type=jnp.float32)  13.2 us
    dot_general x1, matrix products, local(): jnp.einsum('ptf,fc->ptc', lax.all_gather(attended, 'dp', axis=0, tiled=Tr...  12.2 us
    all_gather x1, blocking collectives, local(): lax.all_gather(new_values, 'seq', axis=1, tiled=True)  11.7 us
  transfers between devices with their start and end apart: 6, of which 3 were waited for; matrix products, arithmetic and copies ran while one was open for 6% of the time, Pallas kernels for 0%

commit v1 on v0

--- a/solution.py
+++ b/solution.py
@@ -1,8 +1,11 @@
+import functools
 import math
 
 import jax
 import jax.numpy as jnp
 from jax import lax
+from jax.experimental import pallas as pl
+from jax.experimental.pallas import tpu as pltpu
 from jax.sharding import PartitionSpec as P
 
 HD = 128
@@ -151,6 +154,377 @@
     return lax.all_to_all(summed_cols[:, :, None, :], "dp", split_axis=0, concat_axis=2, tiled=True)
 
 
+MESH = pl.DeviceIdType.MESH
+LANES = 128
+
+
+def fused_kernel(
+    n_seq,
+    n_dp,
+    group,
+    q_ref,
+    nk_ref,
+    nv_ref,
+    ck_ref,
+    cv_ref,
+    meta_ref,
+    w_ref,
+    out_ref,
+    qb,
+    kb,
+    vb,
+    mb,
+    att,
+    rows,
+    wv,
+    acc,
+    half_out,
+    half_in,
+    fin,
+    z_send,
+    z_recv,
+    att_send,
+    att_recv,
+    dp_send,
+    dp_recv,
+    t_send,
+    t_recv,
+    o_send,
+    o_recv,
+    w_sem,
+):
+    s = lax.axis_index("seq")
+    p = lax.axis_index("dp")
+    t = lax.axis_index("tensor")
+    toks = qb.shape[1]
+    width = group * HD
+    slots = ck_ref.shape[1]
+    keys = kb.shape[1]
+    cols = w_ref.shape[1]
+    half = cols // 2
+    scale2 = HD ** (-0.5) * math.log2(math.e)
+
+    def z_parts(d, k):
+        own = pl.ds(pl.multiple_of(d * HD, HD), HD)
+        wide = pl.ds(pl.multiple_of(d * width, width), width)
+        return (
+            (meta_ref, mb.at[k]),
+            (ck_ref.at[0, :, own], kb.at[k, pl.ds(0, slots), :]),
+            (cv_ref.at[0, :, own], vb.at[k, pl.ds(0, slots), :]),
+            (nk_ref.at[0, :, own], kb.at[k, pl.ds(slots, toks), :]),
+            (nv_ref.at[0, :, own], vb.at[k, pl.ds(slots, toks), :]),
+            (q_ref.at[0, :, wide], qb.at[k]),
+        )
+
+    def z_copy(kind, k):
+        d = lax.rem(s + k, n_seq)
+        src, dst = z_parts(d, k)[kind]
+        return pltpu.make_async_remote_copy(
+            src_ref=src,
+            dst_ref=dst,
+            send_sem=z_send.at[kind, k],
+            recv_sem=z_recv.at[kind, k],
+            device_id={"seq": d},
+            device_id_type=MESH,
+        )
+
+    def own_copy(kind):
+        src, dst = z_parts(s, 0)[kind]
+        return pltpu.make_async_copy(src, dst, z_recv.at[kind, 0])
+
+    def att_copy(k):
+        return pltpu.make_async_remote_copy(
+            src_ref=att.at[k],
+            dst_ref=rows.at[k, 0],
+            send_sem=att_send.at[k],
+            recv_sem=att_recv.at[k],
+            device_id={"seq": lax.rem(s + n_seq - k, n_seq)},
+            device_id_type=MESH,
+        )
+
+    def dp_copy(k, j):
+        return pltpu.make_async_remote_copy(
+            src_ref=rows.at[k, 0],
+            dst_ref=rows.at[k, j],
+            send_sem=dp_send.at[k, j],
+            recv_sem=dp_recv.at[k, j],
+            device_id={"dp": lax.rem(p + j, n_dp)},
+            device_id_type=MESH,
+        )
+
+    def out_copy(j):
+        return pltpu.make_async_remote_copy(
+            src_ref=fin.at[j],
+            dst_ref=out_ref.at[p],
+            send_sem=o_send.at[j],
+            recv_sem=o_recv.at[j],
+            device_id={"dp": lax.rem(p + n_dp - j, n_dp)},
+            device_id_type=MESH,
+        )
+
+    def w_copy(k):
+        part = pl.ds(pl.multiple_of(lax.rem(s + k, n_seq) * width, width), width)
+        return pltpu.make_async_copy(w_ref.at[part, :], wv.at[k], w_sem.at[k])
+
+    barrier = pltpu.get_barrier_semaphore()
+    for k in range(1, n_seq):
+        pl.semaphore_signal(
+            barrier, inc=1, device_id={"seq": lax.rem(s + k, n_seq)}, device_id_type=MESH
+        )
+    for j in range(1, n_dp):
+        pl.semaphore_signal(
+            barrier, inc=1, device_id={"dp": lax.rem(p + j, n_dp)}, device_id_type=MESH
+        )
+    pl.semaphore_signal(barrier, inc=1, device_id={"tensor": 1 - t}, device_id_type=MESH)
+    for kind in range(6):
+        own_copy(kind).start()
+    for k in range(n_seq):
+        kb[k, slots + toks :, :] = jnp.zeros((keys - slots - toks, HD), kb.dtype)
+        vb[k, slots + toks :, :] = jnp.zeros((keys - slots - toks, HD), vb.dtype)
+    pl.semaphore_wait(barrier, n_seq + n_dp - 1)
+
+    for kinds in ((0, 1, 2, 3, 4), (5,)):
+        for k in range(1, n_seq):
+            for kind in kinds:
+                z_copy(kind, k).start()
+    for k in range(n_seq):
+        w_copy(k).start()
+    for kind in range(5):
+        own_copy(kind).wait()
+    for k in range(1, n_seq):
+        for kind in range(5):
+            z_copy(kind, k).wait_recv()
+
+    lane = lax.broadcasted_iota(jnp.int32, (toks, keys), 1)
+    token = lax.broadcasted_iota(jnp.int32, (toks, keys), 0)
+    step_heads = max(1, group // 2)
+
+    def attend(k):
+        first = lax.rem(s + n_seq - k, n_seq) * toks
+        doc_row = mb[k, 0:1, slots : slots + LANES]
+        doc_col = jnp.transpose(jnp.broadcast_to(doc_row, (LANES, LANES)))[:toks, 0:1]
+
+        @pl.loop(0, group // step_heads)
+        def _(part):
+            base = pl.multiple_of(part * (step_heads * HD), step_heads * HD)
+            queries = jnp.concatenate(
+                [
+                    qb[k, :, pl.ds(pl.multiple_of(base + i * HD, HD), HD)]
+                    for i in range(step_heads)
+                ],
+                axis=0,
+            )
+            top = weight_sum = summed = None
+            for j in range(n_seq):
+                scores = lax.dot_general(
+                    queries,
+                    kb[j],
+                    (((1,), (1,)), ((), ())),
+                    preferred_element_type=jnp.float32,
+                )
+                fresh_at = lax.rem(s + n_seq - j, n_seq) * toks - slots
+                seen = (mb[j, 0:1, :] == doc_col) & (
+                    (lane < slots) | (lane + fresh_at <= token + first)
+                )
+                bias = jnp.where(seen, 0.0, masked_score)
+                scores = scores + jnp.concatenate([bias] * step_heads, axis=0)
+                group_top = jnp.max(scores, axis=-1, keepdims=True)
+                new_top = group_top if top is None else jnp.maximum(top, group_top)
+                weights = jnp.exp2((scores - new_top) * scale2)
+                part_sum = jnp.sum(weights, axis=-1, keepdims=True)
+                part_out = jnp.dot(
+                    weights.astype(jnp.bfloat16), vb[j], preferred_element_type=jnp.float32
+                )
+                if top is None:
+                    weight_sum, summed = part_sum, part_out
+                else:
+                    factor = jnp.exp2((top - new_top) * scale2)
+                    weight_sum = weight_sum * factor + part_sum
+                    summed = summed * factor + part_out
+                top = new_top
+            result = (summed / weight_sum).astype(jnp.bfloat16)
+            for i in range(step_heads):
+                att[k, :, pl.ds(pl.multiple_of(base + i * HD, HD), HD)] = result[
+                    i * toks : (i + 1) * toks
+                ]
+
+    @pl.loop(0, n_seq)
+    def _(k):
+        @pl.when(k == 0)
+        def _():
+            own_copy(5).wait()
+
+        for other in range(1, n_seq):
+
+            @pl.when(k == other)
+            def _():
+                z_copy(5, other).wait_recv()
+
+        attend(k)
+
+        @pl.when(k == 0)
+        def _():
+            rows[0, 0] = att[0]
+            for j in range(1, n_dp):
+                dp_copy(0, j).start()
+
+        for other in range(1, n_seq):
+
+            @pl.when(k == other)
+            def _():
+                att_copy(other).start()
+
+    tile = math.gcd(half, 512)
+
+    def project(k, n):
+        lhs = rows[k].reshape(n_dp * toks, width)
+        at = pl.ds(pl.multiple_of(n, tile), tile)
+        product = jnp.dot(lhs, wv[k, :, at], preferred_element_type=jnp.float32)
+        if k > 0:
+            product = product + acc[:, at]
+        return product, at
+
+    def project_all(k):
+        w_copy(k).wait()
+        for j in range(1, n_dp):
+            dp_copy(k, j).wait_recv()
+
+        @pl.loop(0, cols // tile)
+        def _(n):
+            product, at = project(k, n * tile)
+            acc[:, at] = product
+
+    def forward(k):
+        att_copy(k).wait_recv()
+        for j in range(1, n_dp):
+            dp_copy(k, j).start()
+
+    project_all(0)
+    for k in range(1, n_seq):
+        forward(k)
+    for k in range(1, n_seq - 1):
+        project_all(k)
+    last = n_seq - 1
+    w_copy(last).wait()
+    for j in range(1, n_dp):
+        dp_copy(last, j).wait_recv()
+    theirs, mine = (1 - t) * half, t * half
+
+    @pl.loop(0, half // tile)
+    def _(n):
+        product, _ = project(last, theirs + n * tile)
+        half_out[:, pl.ds(pl.multiple_of(n * tile, tile), tile)] = product.astype(jnp.bfloat16)
+
+    across = pltpu.make_async_remote_copy(
+        src_ref=half_out,
+        dst_ref=half_in,
+        send_sem=t_send,
+        recv_sem=t_recv,
+        device_id={"tensor": 1 - t},
+        device_id_type=MESH,
+    )
+    across.start()
+
+    @pl.loop(0, half // tile)
+    def _(n):
+        product, at = project(last, mine + n * tile)
+        acc[:, at] = product
+
+    across.wait_recv()
+    own_half = pl.ds(pl.multiple_of(mine, half), half)
+    for j in (*range(1, n_dp), 0):
+        band = pl.ds(j * toks, toks)
+        total = acc[band, own_half] + half_in[band, :].astype(jnp.float32)
+        fin[j] = total.astype(jnp.bfloat16)
+        if j:
+            out_copy(j).start()
+    keep = pltpu.make_async_copy(fin.at[0], out_ref.at[p], o_send.at[0])
+    keep.start()
+
+    for k in range(1, n_seq):
+        for kind in range(6):
+            z_copy(kind, k).wait_send()
+        att_copy(k).wait_send()
+    for k in range(n_seq):
+        for j in range(1, n_dp):
+            dp_copy(k, j).wait_send()
+    across.wait_send()
+    keep.wait()
+    for j in range(1, n_dp):
+        out_copy(j).wait()
+
+
+def fused(
+    n_seq,
+    n_dp,
+    queries,
+    new_keys,
+    new_values,
+    cache_keys,
+    cache_values,
+    keep_lengths,
+    cache_doc,
+    new_doc,
+    out_weight,
+):
+    toks = queries.shape[1]
+    slots = cache_keys.shape[1]
+    cols = out_weight.shape[1]
+    group = queries.shape[2] // cache_keys.shape[2]
+    width = group * HD
+    keys = slots + pl.cdiv(toks, LANES) * LANES
+    position = jnp.arange(slots, dtype=jnp.int32)
+    kept_doc = jnp.where(position < keep_lengths[0, 0], cache_doc[0], -1)
+    pad = jnp.full((keys - slots - toks,), -2, jnp.int32)
+    meta = jnp.concatenate([kept_doc, new_doc[0], pad]).astype(jnp.float32)
+    meta = jnp.broadcast_to(meta[None], (8, keys))
+    dma = pltpu.SemaphoreType.DMA
+    bf16 = jnp.bfloat16
+    blocks = pl.pallas_call(
+        functools.partial(fused_kernel, n_seq, n_dp, group),
+        out_shape=jax.ShapeDtypeStruct((n_dp, toks, cols // 2), bf16),
+        in_specs=[pl.BlockSpec(memory_space=pl.ANY)] * 7,
+        out_specs=pl.BlockSpec(memory_space=pl.ANY),
+        scratch_shapes=[
+            pltpu.VMEM((n_seq, toks, width), bf16),
+            pltpu.VMEM((n_seq, keys, HD), bf16),
+            pltpu.VMEM((n_seq, keys, HD), bf16),
+            pltpu.VMEM((n_seq, 8, keys), jnp.float32),
+            pltpu.VMEM((n_seq, toks, width), bf16),
+            pltpu.VMEM((n_seq, n_dp, toks, width), bf16),
+            pltpu.VMEM((n_seq, width, cols), bf16),
+            pltpu.VMEM((n_dp * toks, cols), jnp.float32),
+            pltpu.VMEM((n_dp * toks, cols // 2), bf16),
+            pltpu.VMEM((n_dp * toks, cols // 2), bf16),
+            pltpu.VMEM((n_dp, toks, cols // 2), bf16),
+            dma((6, n_seq)),
+            dma((6, n_seq)),
+            dma((n_seq,)),
+            dma((n_seq,)),
+            dma((n_seq, n_dp)),
+            dma((n_seq, n_dp)),
+            dma,
+            dma,
+            dma((n_dp,)),
+            dma((n_dp,)),
+            dma((n_seq,)),
+        ],
+        compiler_params=pltpu.CompilerParams(
+            collective_id=0, has_side_effects=True, vmem_limit_bytes=56 << 20
+        ),
+    )(queries, new_keys, new_values, cache_keys, cache_values, meta, out_weight)
+    return blocks.transpose(1, 0, 2)[None]
+
+
+def placed_local(mesh, *args):
+    n_seq, n_dp, n_tensor = (mesh.shape[axis] for axis in ("seq", "dp", "tensor"))
+    queries, cache_keys = args[0], args[3]
+    local_kv = cache_keys.shape[2] // HD
+    if local_kv == n_seq and n_tensor == 2 and queries.shape[1] <= LANES:
+        return fused(n_seq, n_dp, *args)
+    return local(*args)
+
+
 def solution(mesh):
     placed = (
         P("dp", "seq", "tensor"),
@@ -164,5 +538,9 @@
         P("tensor", "dp"),
     )
     return jax.shard_map(
-        local, mesh=mesh, in_specs=placed, out_specs=P("dp", "seq", None, "tensor"), check_vma=False
-    )
+        functools.partial(placed_local, mesh),
+        mesh=mesh,
+        in_specs=placed,
+        out_specs=P("dp", "seq", None, "tensor"),
+        check_vma=False,
+    )

time: 356 us -> 90.2 us (0.25); the launches traced: 351 us -> 90 us
  blocking collectives: 124 us -> 0 us
  waiting for transfers between devices: 90.5 us -> 0 us
  Pallas kernels: 0 us -> 85.1 us
  matrix products: 41.6 us -> 0 us
  local copies, waits for them, and re-layouts: 30 us -> 2.85 us
  other arithmetic: 19.6 us -> 1.42 us
  loops' own time: 15.9 us -> 0 us
  starting transfers between devices: 15.9 us -> 0 us
  between operations: 14.2 us -> 0.66 us
    all_gather x2 -> x0, blocking collectives: 109 us -> none  [the longest x1 97.3 us: local(): lax.all_gather(new_keys, 'seq', axis=1, tiled=True)]
    pallas_call x0 -> x1, Pallas kernels: none -> 85.1 us  [fused(): pl.pallas_call(functools.partial(fused_kernel, n_seq, n_dp, group), out_s...]
    all_gather x2 -> x0, waiting for transfers between devices: 79.1 us -> none  [the longest x1 41.3 us: local(): lax.all_gather(attended, 'dp', axis=0, tiled=True)]
    dot_general x19 -> x0, matrix products: 41.6 us -> none  [the longest x8 13.2 us: softmax_terms(): jnp.dot(weights.astype(jnp.bfloat16), value_rows, preferred_element_type=...]
    another operation x1 -> x0, loops' own time: 15.9 us -> none  [local(): lax.map(block_terms, (query_blocks, doc_blocks, head_ids))]
    all_to_all x3 -> x0, starting transfers between devices: 15.8 us -> none  [the longest x1 5.93 us: local(): lax.all_to_all(cache_sum[None], 'seq', split_axis=2, concat_axis=0, tiled...]
    reduce_scatter x1 -> x0, waiting for transfers between devices: 10.6 us -> none  [local(): lax.psum_scatter(partial_cols, 'tensor', scatter_dimension=2, tiled=True)]
    all_to_all x1 -> x0, blocking collectives: 10.6 us -> none  [local(): lax.all_to_all(summed_cols[:, :, None, :], 'dp', split_axis=0, concat_axi...]
  transfers between devices with their start and end apart: 6 -> 0, of which waited for: 3 -> 0; matrix products, arithmetic and copies ran while one was open for 6% -> 0% of each run, Pallas kernels for 0% -> 0%
where the time goes in v1:
time: 90.2 us; the launch traced here: 90 us
  Pallas kernels  85.1 us (94%)
  local copies, waits for them, and re-layouts  2.85 us (3%)
  other arithmetic  1.42 us (2%)
    pallas_call x1, Pallas kernels, fused(): pl.pallas_call(functools.partial(fused_kernel, n_seq, n_dp, group), out_s...  85.1 us
    broadcast_in_dim x1, local copies, waits for them, and re-layouts, fused(): return blocks.transpose(1, 0, 2)[None]  2.24 us

profile of v1, /device:TPU:25, one launch (start us, length us, event | category | flops | bytes accessed | tf_op | source)
XLA Modules:
  0.0 90.0 jit_solution(8786460800071580848)
XLA Ops:
  0.7 0.7 compare_select_fusion
  1.3 0.7 add_convert_fusion
  2.1 0.6 broadcast_in_dim.18.meta_ref
  2.7 85.1 %shard_map.91 = bf16[4,64,1024]{2,1,0:T(8,128)(2,1)} custom-call(bf16[1,64,4096]{2,1,0:T(8,128)(2,1)} %q_ref.1, bf16[1,64,512]{2,1,0:T(8,128)(2,1)} %nk_ref.1, bf16[1,64,512]{2,1,0:T(8,128)(2,1)} %nv_ref.1, bf16[1,512,512]{2,1,0:T(8,128)(2,1)} %ck_ref.1, bf16[1,512,512]{2,1,0:T(8,128)(2,1)} %cv_ref.1, f32[8,640]{1,0:T(8,128)} %broadcast_in_dim.18.meta_ref, ...), custom_call_target="tpu_custom_call" | custom-call | tf_op jit(solution)/shard_map/pallas_call | solution.py:483
  87.8 2.2 %copy.10 = bf16[1,64,4,1024]{3,2,1,0:T(4,128)(2,1)} copy(bf16[1,64,4,1024]{3,1,2,0:T(8,128)(2,1)} %bitcast.7) | data formatting | bytes 1048576 | tf_op jit(solution)/shard_map/broadcast_in_dim | solution.py:516
  (1 shorter events, 0.0 us)

commit v2 on v1

--- a/solution.py
+++ b/solution.py
@@ -156,6 +156,7 @@
 
 MESH = pl.DeviceIdType.MESH
 LANES = 128
+PARTS = 2
 
 
 def fused_kernel(
@@ -167,7 +168,9 @@
     nv_ref,
     ck_ref,
     cv_ref,
-    meta_ref,
+    keep_ref,
+    cache_doc_ref,
+    new_doc_ref,
     w_ref,
     out_ref,
     qb,
@@ -202,13 +205,15 @@
     keys = kb.shape[1]
     cols = w_ref.shape[1]
     half = cols // 2
+    tile = half // fin.shape[0]
+    depth = width // PARTS
     scale2 = HD ** (-0.5) * math.log2(math.e)
 
     def z_parts(d, k):
         own = pl.ds(pl.multiple_of(d * HD, HD), HD)
         wide = pl.ds(pl.multiple_of(d * width, width), width)
         return (
-            (meta_ref, mb.at[k]),
+            (mb.at[0], mb.at[k]),
             (ck_ref.at[0, :, own], kb.at[k, pl.ds(0, slots), :]),
             (cv_ref.at[0, :, own], vb.at[k, pl.ds(0, slots), :]),
             (nk_ref.at[0, :, own], kb.at[k, pl.ds(slots, toks), :]),
@@ -232,32 +237,32 @@
         src, dst = z_parts(s, 0)[kind]
         return pltpu.make_async_copy(src, dst, z_recv.at[kind, 0])
 
-    def att_copy(k):
+    def att_copy(k, part):
         return pltpu.make_async_remote_copy(
-            src_ref=att.at[k],
-            dst_ref=rows.at[k, 0],
-            send_sem=att_send.at[k],
-            recv_sem=att_recv.at[k],
+            src_ref=att.at[k, part],
+            dst_ref=rows.at[k, part, 0],
+            send_sem=att_send.at[k, part],
+            recv_sem=att_recv.at[k, part],
             device_id={"seq": lax.rem(s + n_seq - k, n_seq)},
             device_id_type=MESH,
         )
 
-    def dp_copy(k, j):
+    def dp_copy(k, part, j):
         return pltpu.make_async_remote_copy(
-            src_ref=rows.at[k, 0],
-            dst_ref=rows.at[k, j],
-            send_sem=dp_send.at[k, j],
-            recv_sem=dp_recv.at[k, j],
+            src_ref=rows.at[k, part, 0],
+            dst_ref=rows.at[k, part, j],
+            send_sem=dp_send.at[k, part, j],
+            recv_sem=dp_recv.at[k, part, j],
             device_id={"dp": lax.rem(p + j, n_dp)},
             device_id_type=MESH,
         )
 
-    def out_copy(j):
+    def out_copy(n, j):
         return pltpu.make_async_remote_copy(
-            src_ref=fin.at[j],
-            dst_ref=out_ref.at[p],
-            send_sem=o_send.at[j],
-            recv_sem=o_recv.at[j],
+            src_ref=fin.at[n, j],
+            dst_ref=out_ref.at[p, :, pl.ds(n * tile, tile)],
+            send_sem=o_send.at[n, j],
+            recv_sem=o_recv.at[n, j],
             device_id={"dp": lax.rem(p + n_dp - j, n_dp)},
             device_id_type=MESH,
         )
@@ -276,182 +281,179 @@
             barrier, inc=1, device_id={"dp": lax.rem(p + j, n_dp)}, device_id_type=MESH
         )
     pl.semaphore_signal(barrier, inc=1, device_id={"tensor": 1 - t}, device_id_type=MESH)
-    for kind in range(6):
+    for kind in range(1, 6):
         own_copy(kind).start()
+    place = lax.broadcasted_iota(jnp.int32, (1, slots), 1)
+    kept_doc = jnp.where(place < keep_ref[0, 0], cache_doc_ref[...], -1)
+    mb[0, :, :slots] = kept_doc.astype(jnp.float32)
+    mb[0, :, slots:] = jnp.full((1, keys - slots), -2.0, jnp.float32)
+    mb[0, :, slots : slots + toks] = new_doc_ref[...].astype(jnp.float32)
     for k in range(n_seq):
         kb[k, slots + toks :, :] = jnp.zeros((keys - slots - toks, HD), kb.dtype)
         vb[k, slots + toks :, :] = jnp.zeros((keys - slots - toks, HD), vb.dtype)
     pl.semaphore_wait(barrier, n_seq + n_dp - 1)
 
-    for kinds in ((0, 1, 2, 3, 4), (5,)):
+    for kinds in ((1, 2, 3, 4, 0), (5,)):
         for k in range(1, n_seq):
             for kind in kinds:
                 z_copy(kind, k).start()
     for k in range(n_seq):
         w_copy(k).start()
-    for kind in range(5):
-        own_copy(kind).wait()
-    for k in range(1, n_seq):
-        for kind in range(5):
-            z_copy(kind, k).wait_recv()
 
     lane = lax.broadcasted_iota(jnp.int32, (toks, keys), 1)
     token = lax.broadcasted_iota(jnp.int32, (toks, keys), 0)
-    step_heads = max(1, group // 2)
-
-    def attend(k):
+    step_heads = group // PARTS
+
+    def attend(k, part, wait_shards):
         first = lax.rem(s + n_seq - k, n_seq) * toks
-        doc_row = mb[k, 0:1, slots : slots + LANES]
+        base = part * depth
+        queries = jnp.concatenate(
+            [qb[k, :, pl.ds(pl.multiple_of(base + i * HD, HD), HD)] for i in range(step_heads)],
+            axis=0,
+        )
+        doc_row = mb[k, :, slots : slots + LANES]
         doc_col = jnp.transpose(jnp.broadcast_to(doc_row, (LANES, LANES)))[:toks, 0:1]
-
-        @pl.loop(0, group // step_heads)
+        top = weight_sum = summed = None
+        for j in range(n_seq):
+            if wait_shards:
+                for kind in range(5):
+                    if j:
+                        z_copy(kind, j).wait_recv()
+                    elif kind:
+                        own_copy(kind).wait()
+            scores = lax.dot_general(
+                queries,
+                kb[j],
+                (((1,), (1,)), ((), ())),
+                preferred_element_type=jnp.float32,
+            )
+            fresh_at = lax.rem(s + n_seq - j, n_seq) * toks - slots
+            seen = (mb[j] == doc_col) & ((lane < slots) | (lane + fresh_at <= token + first))
+            bias = jnp.where(seen, 0.0, masked_score)
+            scores = scores + jnp.concatenate([bias] * step_heads, axis=0)
+            group_top = jnp.max(scores, axis=-1, keepdims=True)
+            new_top = group_top if top is None else jnp.maximum(top, group_top)
+            weights = jnp.exp2((scores - new_top) * scale2)
+            part_sum = jnp.sum(weights, axis=-1, keepdims=True)
+            part_out = jnp.dot(
+                weights.astype(jnp.bfloat16), vb[j], preferred_element_type=jnp.float32
+            )
+            if top is None:
+                weight_sum, summed = part_sum, part_out
+            else:
+                factor = jnp.exp2((top - new_top) * scale2)
+                weight_sum = weight_sum * factor + part_sum
+                summed = summed * factor + part_out
+            top = new_top
+        result = (summed / weight_sum).astype(jnp.bfloat16)
+        for i in range(step_heads):
+            piece = result[i * toks : (i + 1) * toks]
+            if wait_shards is None:
+                att[k, part, :, i * HD : (i + 1) * HD] = piece
+            else:
+                rows[0, part, 0, :, i * HD : (i + 1) * HD] = piece
+
+    def forward(k, part):
+        if k:
+            att_copy(k, part).wait_recv()
+        for j in range(1, n_dp):
+            dp_copy(k, part, j).start()
+
+    own_copy(5).wait()
+    for part in range(PARTS):
+        attend(0, part, part == 0)
+        forward(0, part)
+    for k in range(1, n_seq):
+        z_copy(5, k).wait_recv()
+
+        @pl.loop(0, PARTS)
         def _(part):
-            base = pl.multiple_of(part * (step_heads * HD), step_heads * HD)
-            queries = jnp.concatenate(
-                [
-                    qb[k, :, pl.ds(pl.multiple_of(base + i * HD, HD), HD)]
-                    for i in range(step_heads)
-                ],
-                axis=0,
-            )
-            top = weight_sum = summed = None
-            for j in range(n_seq):
-                scores = lax.dot_general(
-                    queries,
-                    kb[j],
-                    (((1,), (1,)), ((), ())),
-                    preferred_element_type=jnp.float32,
-                )
-                fresh_at = lax.rem(s + n_seq - j, n_seq) * toks - slots
-                seen = (mb[j, 0:1, :] == doc_col) & (
-                    (lane < slots) | (lane + fresh_at <= token + first)
-                )
-                bias = jnp.where(seen, 0.0, masked_score)
-                scores = scores + jnp.concatenate([bias] * step_heads, axis=0)
-                group_top = jnp.max(scores, axis=-1, keepdims=True)
-                new_top = group_top if top is None else jnp.maximum(top, group_top)
-                weights = jnp.exp2((scores - new_top) * scale2)
-                part_sum = jnp.sum(weights, axis=-1, keepdims=True)
-                part_out = jnp.dot(
-                    weights.astype(jnp.bfloat16), vb[j], preferred_element_type=jnp.float32
-                )
-                if top is None:
-                    weight_sum, summed = part_sum, part_out
-                else:
-                    factor = jnp.exp2((top - new_top) * scale2)
-                    weight_sum = weight_sum * factor + part_sum
-                    summed = summed * factor + part_out
-                top = new_top
-            result = (summed / weight_sum).astype(jnp.bfloat16)
-            for i in range(step_heads):
-                att[k, :, pl.ds(pl.multiple_of(base + i * HD, HD), HD)] = result[
-                    i * toks : (i + 1) * toks
-                ]
-
-    @pl.loop(0, n_seq)
-    def _(k):
-        @pl.when(k == 0)
-        def _():
-            own_copy(5).wait()
-
-        for other in range(1, n_seq):
-
-            @pl.when(k == other)
-            def _():
-                z_copy(5, other).wait_recv()
-
-        attend(k)
-
-        @pl.when(k == 0)
-        def _():
-            rows[0, 0] = att[0]
-            for j in range(1, n_dp):
-                dp_copy(0, j).start()
-
-        for other in range(1, n_seq):
-
-            @pl.when(k == other)
-            def _():
-                att_copy(other).start()
-
-    tile = math.gcd(half, 512)
-
-    def project(k, n):
-        lhs = rows[k].reshape(n_dp * toks, width)
+            attend(k, part, None)
+            att_copy(k, part).start()
+
+        if k > 1:
+            for part in range(PARTS):
+                forward(k - 1, part)
+
+    def project(k, part, n):
+        lhs = rows[k, part].reshape(n_dp * toks, depth)
         at = pl.ds(pl.multiple_of(n, tile), tile)
-        product = jnp.dot(lhs, wv[k, :, at], preferred_element_type=jnp.float32)
-        if k > 0:
+        deep = pl.ds(part * depth, depth)
+        product = jnp.dot(lhs, wv[k, deep, at], preferred_element_type=jnp.float32)
+        if k or part:
             product = product + acc[:, at]
         return product, at
 
-    def project_all(k):
-        w_copy(k).wait()
+    def ready(k, part):
+        if part == 0:
+            w_copy(k).wait()
         for j in range(1, n_dp):
-            dp_copy(k, j).wait_recv()
+            dp_copy(k, part, j).wait_recv()
+
+    def project_all(k, part):
+        ready(k, part)
 
         @pl.loop(0, cols // tile)
         def _(n):
-            product, at = project(k, n * tile)
+            product, at = project(k, part, n * tile)
             acc[:, at] = product
 
-    def forward(k):
-        att_copy(k).wait_recv()
-        for j in range(1, n_dp):
-            dp_copy(k, j).start()
-
-    project_all(0)
+    last = (n_seq - 1, PARTS - 1)
+    project_all(0, 0)
+    forward(last[0], 0)
+    project_all(0, 1)
+    for part in range(1, PARTS):
+        forward(last[0], part)
     for k in range(1, n_seq):
-        forward(k)
-    for k in range(1, n_seq - 1):
-        project_all(k)
-    last = n_seq - 1
-    w_copy(last).wait()
-    for j in range(1, n_dp):
-        dp_copy(last, j).wait_recv()
+        for part in range(PARTS):
+            if (k, part) != last:
+                project_all(k, part)
+    ready(*last)
     theirs, mine = (1 - t) * half, t * half
 
-    @pl.loop(0, half // tile)
-    def _(n):
-        product, _ = project(last, theirs + n * tile)
-        half_out[:, pl.ds(pl.multiple_of(n * tile, tile), tile)] = product.astype(jnp.bfloat16)
-
-    across = pltpu.make_async_remote_copy(
-        src_ref=half_out,
-        dst_ref=half_in,
-        send_sem=t_send,
-        recv_sem=t_recv,
-        device_id={"tensor": 1 - t},
-        device_id_type=MESH,
-    )
-    across.start()
-
-    @pl.loop(0, half // tile)
-    def _(n):
-        product, at = project(last, mine + n * tile)
-        acc[:, at] = product
-
-    across.wait_recv()
-    own_half = pl.ds(pl.multiple_of(mine, half), half)
-    for j in (*range(1, n_dp), 0):
-        band = pl.ds(j * toks, toks)
-        total = acc[band, own_half] + half_in[band, :].astype(jnp.float32)
-        fin[j] = total.astype(jnp.bfloat16)
-        if j:
-            out_copy(j).start()
-    keep = pltpu.make_async_copy(fin.at[0], out_ref.at[p], o_send.at[0])
-    keep.start()
+    def across(n):
+        return pltpu.make_async_remote_copy(
+            src_ref=half_out.at[n],
+            dst_ref=half_in.at[n],
+            send_sem=t_send.at[n],
+            recv_sem=t_recv.at[n],
+            device_id={"tensor": 1 - t},
+            device_id_type=MESH,
+        )
+
+    def keep(n):
+        there = out_ref.at[p, :, pl.ds(n * tile, tile)]
+        return pltpu.make_async_copy(fin.at[n, 0], there, o_send.at[n, 0])
+
+    tiles = half // tile
+    for n in range(tiles):
+        product, _ = project(*last, theirs + n * tile)
+        half_out[n] = product.astype(jnp.bfloat16)
+        across(n).start()
+    for n in range(tiles):
+        product, _ = project(*last, mine + n * tile)
+        across(n).wait_recv()
+        total = (product + half_in[n].astype(jnp.float32)).astype(jnp.bfloat16)
+        for j in (*range(1, n_dp), 0):
+            fin[n, j] = total[j * toks : (j + 1) * toks]
+            if j:
+                out_copy(n, j).start()
+        keep(n).start()
 
     for k in range(1, n_seq):
         for kind in range(6):
             z_copy(kind, k).wait_send()
-        att_copy(k).wait_send()
+        for part in range(PARTS):
+            att_copy(k, part).wait_send()
     for k in range(n_seq):
+        for part in range(PARTS):
+            for j in range(1, n_dp):
+                dp_copy(k, part, j).wait_send()
+    for n in range(tiles):
+        across(n).wait_send()
+        keep(n).wait()
         for j in range(1, n_dp):
-            dp_copy(k, j).wait_send()
-    across.wait_send()
-    keep.wait()
-    for j in range(1, n_dp):
-        out_copy(j).wait()
+            out_copy(n, j).wait()
 
 
 def fused(
@@ -473,46 +475,48 @@
     group = queries.shape[2] // cache_keys.shape[2]
     width = group * HD
     keys = slots + pl.cdiv(toks, LANES) * LANES
-    position = jnp.arange(slots, dtype=jnp.int32)
-    kept_doc = jnp.where(position < keep_lengths[0, 0], cache_doc[0], -1)
-    pad = jnp.full((keys - slots - toks,), -2, jnp.int32)
-    meta = jnp.concatenate([kept_doc, new_doc[0], pad]).astype(jnp.float32)
-    meta = jnp.broadcast_to(meta[None], (8, keys))
+    tiles = 2
     dma = pltpu.SemaphoreType.DMA
     bf16 = jnp.bfloat16
     blocks = pl.pallas_call(
         functools.partial(fused_kernel, n_seq, n_dp, group),
         out_shape=jax.ShapeDtypeStruct((n_dp, toks, cols // 2), bf16),
-        in_specs=[pl.BlockSpec(memory_space=pl.ANY)] * 7,
+        in_specs=[pl.BlockSpec(memory_space=pl.ANY)] * 5
+        + [
+            pl.BlockSpec(memory_space=pltpu.SMEM),
+            pl.BlockSpec(memory_space=pltpu.VMEM),
+            pl.BlockSpec(memory_space=pltpu.VMEM),
+            pl.BlockSpec(memory_space=pl.ANY),
+        ],
         out_specs=pl.BlockSpec(memory_space=pl.ANY),
         scratch_shapes=[
             pltpu.VMEM((n_seq, toks, width), bf16),
             pltpu.VMEM((n_seq, keys, HD), bf16),
             pltpu.VMEM((n_seq, keys, HD), bf16),
-            pltpu.VMEM((n_seq, 8, keys), jnp.float32),
-            pltpu.VMEM((n_seq, toks, width), bf16),
-            pltpu.VMEM((n_seq, n_dp, toks, width), bf16),
+            pltpu.VMEM((n_seq, 1, keys), jnp.float32),
+            pltpu.VMEM((n_seq, PARTS, toks, width // PARTS), bf16),
+            pltpu.VMEM((n_seq, PARTS, n_dp, toks, width // PARTS), bf16),
             pltpu.VMEM((n_seq, width, cols), bf16),
             pltpu.VMEM((n_dp * toks, cols), jnp.float32),
-            pltpu.VMEM((n_dp * toks, cols // 2), bf16),
-            pltpu.VMEM((n_dp * toks, cols // 2), bf16),
-            pltpu.VMEM((n_dp, toks, cols // 2), bf16),
+            pltpu.VMEM((tiles, n_dp * toks, cols // 2 // tiles), bf16),
+            pltpu.VMEM((tiles, n_dp * toks, cols // 2 // tiles), bf16),
+            pltpu.VMEM((tiles, n_dp, toks, cols // 2 // tiles), bf16),
             dma((6, n_seq)),
             dma((6, n_seq)),
-            dma((n_seq,)),
-            dma((n_seq,)),
-            dma((n_seq, n_dp)),
-            dma((n_seq, n_dp)),
-            dma,
-            dma,
-            dma((n_dp,)),
-            dma((n_dp,)),
+            dma((n_seq, PARTS)),
+            dma((n_seq, PARTS)),
+            dma((n_seq, PARTS, n_dp)),
+            dma((n_seq, PARTS, n_dp)),
+            dma((tiles,)),
+            dma((tiles,)),
+            dma((tiles, n_dp)),
+            dma((tiles, n_dp)),
             dma((n_seq,)),
         ],
         compiler_params=pltpu.CompilerParams(
             collective_id=0, has_side_effects=True, vmem_limit_bytes=56 << 20
         ),
-    )(queries, new_keys, new_values, cache_keys, cache_values, meta, out_weight)
+    )(queries, new_keys, new_values, cache_keys, cache_values, keep_lengths, cache_doc, new_doc, out_weight)
     return blocks.transpose(1, 0, 2)[None]
 
 

time: 90.2 us -> 82.8 us (0.918)
  Pallas kernels: 85.1 us -> 79.2 us
  other arithmetic: 1.42 us -> 0 us
    pallas_call x1, Pallas kernels: 85.1 us -> 79.2 us  [fused(): pl.pallas_call(functools.partial(fused_kernel, n_seq, n_dp, group), out_s...]
where the time goes in v2:
time: 82.8 us; the launch traced here: 82.1 us
  Pallas kernels  79.2 us (96%)
  local copies, waits for them, and re-layouts  2.24 us (3%)
    pallas_call x1, Pallas kernels, fused(): pl.pallas_call(functools.partial(fused_kernel, n_seq, n_dp, group), out_s...  79.2 us
    broadcast_in_dim x1, local copies, waits for them, and re-layouts, fused(): return blocks.transpose(1, 0, 2)[None]  2.24 us

profile of v2, /device:TPU:25, one launch (start us, length us, event | category | flops | bytes accessed | tf_op | source)
XLA Modules:
  0.0 82.1 jit_solution(4422861375155491644)
XLA Ops:
  0.7 79.2 %shard_map.91 = bf16[4,64,1024]{2,1,0:T(8,128)(2,1)} custom-call(bf16[1,64,4096]{2,1,0:T(8,128)(2,1)} %q_ref.1, bf16[1,64,512]{2,1,0:T(8,128)(2,1)} %nk_ref.1, bf16[1,64,512]{2,1,0:T(8,128)(2,1)} %nv_ref.1, bf16[1,512,512]{2,1,0:T(8,128)(2,1)} %ck_ref.1, bf16[1,512,512]{2,1,0:T(8,128)(2,1)} %cv_ref.1, s32[1,1]{1,0:T(1,128)S(6)} %copy.11.keep_ref, ...), custom_call_target="tpu_custom_call" | custom-call | tf_op jit(solution)/shard_map/pallas_call | solution.py:481
  79.9 2.2 %copy.10 = bf16[1,64,4,1024]{3,2,1,0:T(4,128)(2,1)} copy(bf16[1,64,4,1024]{3,1,2,0:T(8,128)(2,1)} %bitcast.3) | data formatting | bytes 1048576 | tf_op jit(solution)/shard_map/broadcast_in_dim | solution.py:520

commit v3 on v2

--- a/solution.py
+++ b/solution.py
@@ -199,14 +199,15 @@
     s = lax.axis_index("seq")
     p = lax.axis_index("dp")
     t = lax.axis_index("tensor")
-    toks = qb.shape[1]
+    part_toks = qb.shape[2]
+    toks = PARTS * part_toks
     width = group * HD
     slots = ck_ref.shape[1]
     keys = kb.shape[1]
     cols = w_ref.shape[1]
     half = cols // 2
-    tile = half // fin.shape[0]
-    depth = width // PARTS
+    tiles = fin.shape[1]
+    tile = half // tiles
     scale2 = HD ** (-0.5) * math.log2(math.e)
 
     def z_parts(d, k):
@@ -218,7 +219,10 @@
             (cv_ref.at[0, :, own], vb.at[k, pl.ds(0, slots), :]),
             (nk_ref.at[0, :, own], kb.at[k, pl.ds(slots, toks), :]),
             (nv_ref.at[0, :, own], vb.at[k, pl.ds(slots, toks), :]),
-            (q_ref.at[0, :, wide], qb.at[k]),
+            *(
+                (q_ref.at[0, pl.ds(part * part_toks, part_toks), wide], qb.at[k, part])
+                for part in range(PARTS)
+            ),
         )
 
     def z_copy(kind, k):
@@ -257,12 +261,15 @@
             device_id_type=MESH,
         )
 
-    def out_copy(n, j):
+    def out_place(part, n):
+        return out_ref.at[p, pl.ds(part * part_toks, part_toks), pl.ds(n * tile, tile)]
+
+    def out_copy(part, n, j):
         return pltpu.make_async_remote_copy(
-            src_ref=fin.at[n, j],
-            dst_ref=out_ref.at[p, :, pl.ds(n * tile, tile)],
-            send_sem=o_send.at[n, j],
-            recv_sem=o_recv.at[n, j],
+            src_ref=fin.at[part, n, j],
+            dst_ref=out_place(part, n),
+            send_sem=o_send.at[part, n, j],
+            recv_sem=o_recv.at[part, n, j],
             device_id={"dp": lax.rem(p + n_dp - j, n_dp)},
             device_id_type=MESH,
         )
@@ -281,7 +288,7 @@
             barrier, inc=1, device_id={"dp": lax.rem(p + j, n_dp)}, device_id_type=MESH
         )
     pl.semaphore_signal(barrier, inc=1, device_id={"tensor": 1 - t}, device_id_type=MESH)
-    for kind in range(1, 6):
+    for kind in range(1, 5 + PARTS):
         own_copy(kind).start()
     place = lax.broadcasted_iota(jnp.int32, (1, slots), 1)
     kept_doc = jnp.where(place < keep_ref[0, 0], cache_doc_ref[...], -1)
@@ -297,22 +304,22 @@
         for k in range(1, n_seq):
             for kind in kinds:
                 z_copy(kind, k).start()
+    for part in range(1, PARTS):
+        z_copy(5 + part, 1).start()
     for k in range(n_seq):
         w_copy(k).start()
 
-    lane = lax.broadcasted_iota(jnp.int32, (toks, keys), 1)
-    token = lax.broadcasted_iota(jnp.int32, (toks, keys), 0)
-    step_heads = group // PARTS
-
-    def attend(k, part, wait_shards):
-        first = lax.rem(s + n_seq - k, n_seq) * toks
-        base = part * depth
+    lane = lax.broadcasted_iota(jnp.int32, (part_toks, keys), 1)
+    token = lax.broadcasted_iota(jnp.int32, (part_toks, keys), 0)
+
+    def attend(k, part, into, wait_shards=False):
+        first = lax.rem(s + n_seq - k, n_seq) * toks + part * part_toks
         queries = jnp.concatenate(
-            [qb[k, :, pl.ds(pl.multiple_of(base + i * HD, HD), HD)] for i in range(step_heads)],
-            axis=0,
+            [qb[k, part, :, i * HD : (i + 1) * HD] for i in range(group)], axis=0
         )
         doc_row = mb[k, :, slots : slots + LANES]
-        doc_col = jnp.transpose(jnp.broadcast_to(doc_row, (LANES, LANES)))[:toks, 0:1]
+        doc_col = jnp.transpose(jnp.broadcast_to(doc_row, (LANES, LANES)))
+        doc_col = doc_col[part * part_toks : (part + 1) * part_toks, 0:1]
         top = weight_sum = summed = None
         for j in range(n_seq):
             if wait_shards:
@@ -330,7 +337,7 @@
             fresh_at = lax.rem(s + n_seq - j, n_seq) * toks - slots
             seen = (mb[j] == doc_col) & ((lane < slots) | (lane + fresh_at <= token + first))
             bias = jnp.where(seen, 0.0, masked_score)
-            scores = scores + jnp.concatenate([bias] * step_heads, axis=0)
+            scores = scores + jnp.concatenate([bias] * group, axis=0)
             group_top = jnp.max(scores, axis=-1, keepdims=True)
             new_top = group_top if top is None else jnp.maximum(top, group_top)
             weights = jnp.exp2((scores - new_top) * scale2)
@@ -346,42 +353,45 @@
                 summed = summed * factor + part_out
             top = new_top
         result = (summed / weight_sum).astype(jnp.bfloat16)
-        for i in range(step_heads):
-            piece = result[i * toks : (i + 1) * toks]
-            if wait_shards is None:
-                att[k, part, :, i * HD : (i + 1) * HD] = piece
-            else:
-                rows[0, part, 0, :, i * HD : (i + 1) * HD] = piece
+        for i in range(group):
+            into[:, i * HD : (i + 1) * HD] = result[i * part_toks : (i + 1) * part_toks]
 
     def forward(k, part):
-        if k:
-            att_copy(k, part).wait_recv()
         for j in range(1, n_dp):
             dp_copy(k, part, j).start()
 
-    own_copy(5).wait()
+    def pass_on(k, part):
+        att_copy(k, part).wait_recv()
+        forward(k, part)
+
+    last = n_seq - 1
     for part in range(PARTS):
-        attend(0, part, part == 0)
+        own_copy(5 + part).wait()
+        attend(0, part, rows.at[0, part, 0], wait_shards=part == 0)
         forward(0, part)
-    for k in range(1, n_seq):
-        z_copy(5, k).wait_recv()
-
-        @pl.loop(0, PARTS)
-        def _(part):
-            attend(k, part, None)
+    for part in range(PARTS):
+
+        @pl.loop(1, n_seq)
+        def _(k):
+            z_copy(5 + part, k).wait_recv()
+            attend(k, part, att.at[k, part])
             att_copy(k, part).start()
-
-        if k > 1:
-            for part in range(PARTS):
-                forward(k - 1, part)
+            if part == 0:
+
+                @pl.when(k < last)
+                def _():
+                    for later in range(1, PARTS):
+                        z_copy(5 + later, k + 1).start()
+
+            if part:
+                pass_on(k, part - 1)
 
     def project(k, part, n):
-        lhs = rows[k, part].reshape(n_dp * toks, depth)
+        lhs = rows[k, part].reshape(n_dp * part_toks, width)
         at = pl.ds(pl.multiple_of(n, tile), tile)
-        deep = pl.ds(part * depth, depth)
-        product = jnp.dot(lhs, wv[k, deep, at], preferred_element_type=jnp.float32)
-        if k or part:
-            product = product + acc[:, at]
+        product = jnp.dot(lhs, wv[k, :, at], preferred_element_type=jnp.float32)
+        if k:
+            product = product + acc[part, :, at]
         return product, at
 
     def ready(k, part):
@@ -396,52 +406,50 @@
         @pl.loop(0, cols // tile)
         def _(n):
             product, at = project(k, part, n * tile)
-            acc[:, at] = product
-
-    last = (n_seq - 1, PARTS - 1)
-    project_all(0, 0)
-    forward(last[0], 0)
-    project_all(0, 1)
-    for part in range(1, PARTS):
-        forward(last[0], part)
-    for k in range(1, n_seq):
-        for part in range(PARTS):
-            if (k, part) != last:
-                project_all(k, part)
-    ready(*last)
+            acc[part, :, at] = product
+
     theirs, mine = (1 - t) * half, t * half
 
-    def across(n):
+    def across(part, n):
         return pltpu.make_async_remote_copy(
-            src_ref=half_out.at[n],
-            dst_ref=half_in.at[n],
-            send_sem=t_send.at[n],
-            recv_sem=t_recv.at[n],
+            src_ref=half_out.at[part, n],
+            dst_ref=half_in.at[part, n],
+            send_sem=t_send.at[part, n],
+            recv_sem=t_recv.at[part, n],
             device_id={"tensor": 1 - t},
             device_id_type=MESH,
         )
 
-    def keep(n):
-        there = out_ref.at[p, :, pl.ds(n * tile, tile)]
-        return pltpu.make_async_copy(fin.at[n, 0], there, o_send.at[n, 0])
-
-    tiles = half // tile
-    for n in range(tiles):
-        product, _ = project(*last, theirs + n * tile)
-        half_out[n] = product.astype(jnp.bfloat16)
-        across(n).start()
-    for n in range(tiles):
-        product, _ = project(*last, mine + n * tile)
-        across(n).wait_recv()
-        total = (product + half_in[n].astype(jnp.float32)).astype(jnp.bfloat16)
-        for j in (*range(1, n_dp), 0):
-            fin[n, j] = total[j * toks : (j + 1) * toks]
-            if j:
-                out_copy(n, j).start()
-        keep(n).start()
+    def keep(part, n):
+        return pltpu.make_async_copy(
+            fin.at[part, n, 0], out_place(part, n), o_send.at[part, n, 0]
+        )
+
+    def finish(part):
+        ready(last, part)
+        for n in range(tiles):
+            product, _ = project(last, part, theirs + n * tile)
+            half_out[part, n] = product.astype(jnp.bfloat16)
+            across(part, n).start()
+        for n in range(tiles):
+            product, _ = project(last, part, mine + n * tile)
+            across(part, n).wait_recv()
+            total = (product + half_in[part, n].astype(jnp.float32)).astype(jnp.bfloat16)
+            for j in (*range(1, n_dp), 0):
+                fin[part, n, j] = total[j * part_toks : (j + 1) * part_toks]
+                if j:
+                    out_copy(part, n, j).start()
+            keep(part, n).start()
+
+    for part in range(PARTS):
+        for k in range(last):
+            project_all(k, part)
+            if part == 0:
+                pass_on(k + 1, PARTS - 1)
+        finish(part)
 
     for k in range(1, n_seq):
-        for kind in range(6):
+        for kind in range(5 + PARTS):
             z_copy(kind, k).wait_send()
         for part in range(PARTS):
             att_copy(k, part).wait_send()
@@ -449,11 +457,12 @@
         for part in range(PARTS):
             for j in range(1, n_dp):
                 dp_copy(k, part, j).wait_send()
-    for n in range(tiles):
-        across(n).wait_send()
-        keep(n).wait()
-        for j in range(1, n_dp):
-            out_copy(n, j).wait()
+    for part in range(PARTS):
+        for n in range(tiles):
+            across(part, n).wait_send()
+            keep(part, n).wait()
+            for j in range(1, n_dp):
+                out_copy(part, n, j).wait()
 
 
 def fused(
@@ -476,6 +485,7 @@
     width = group * HD
     keys = slots + pl.cdiv(toks, LANES) * LANES
     tiles = 2
+    part_toks = toks // PARTS
     dma = pltpu.SemaphoreType.DMA
     bf16 = jnp.bfloat16
     blocks = pl.pallas_call(
@@ -490,27 +500,27 @@
         ],
         out_specs=pl.BlockSpec(memory_space=pl.ANY),
         scratch_shapes=[
-            pltpu.VMEM((n_seq, toks, width), bf16),
+            pltpu.VMEM((n_seq, PARTS, part_toks, width), bf16),
             pltpu.VMEM((n_seq, keys, HD), bf16),
             pltpu.VMEM((n_seq, keys, HD), bf16),
             pltpu.VMEM((n_seq, 1, keys), jnp.float32),
-            pltpu.VMEM((n_seq, PARTS, toks, width // PARTS), bf16),
-            pltpu.VMEM((n_seq, PARTS, n_dp, toks, width // PARTS), bf16),
+            pltpu.VMEM((n_seq, PARTS, part_toks, width), bf16),
+            pltpu.VMEM((n_seq, PARTS, n_dp, part_toks, width), bf16),
             pltpu.VMEM((n_seq, width, cols), bf16),
-            pltpu.VMEM((n_dp * toks, cols), jnp.float32),
-            pltpu.VMEM((tiles, n_dp * toks, cols // 2 // tiles), bf16),
-            pltpu.VMEM((tiles, n_dp * toks, cols // 2 // tiles), bf16),
-            pltpu.VMEM((tiles, n_dp, toks, cols // 2 // tiles), bf16),
-            dma((6, n_seq)),
-            dma((6, n_seq)),
+            pltpu.VMEM((PARTS, n_dp * part_toks, cols), jnp.float32),
+            pltpu.VMEM((PARTS, tiles, n_dp * part_toks, cols // 2 // tiles), bf16),
+            pltpu.VMEM((PARTS, tiles, n_dp * part_toks, cols // 2 // tiles), bf16),
+            pltpu.VMEM((PARTS, tiles, n_dp, part_toks, cols // 2 // tiles), bf16),
+            dma((5 + PARTS, n_seq)),
+            dma((5 + PARTS, n_seq)),
             dma((n_seq, PARTS)),
             dma((n_seq, PARTS)),
             dma((n_seq, PARTS, n_dp)),
             dma((n_seq, PARTS, n_dp)),
-            dma((tiles,)),
-            dma((tiles,)),
-            dma((tiles, n_dp)),
-            dma((tiles, n_dp)),
+            dma((PARTS, tiles)),
+            dma((PARTS, tiles)),
+            dma((PARTS, tiles, n_dp)),
+            dma((PARTS, tiles, n_dp)),
             dma((n_seq,)),
         ],
         compiler_params=pltpu.CompilerParams(

time: 82.8 us -> 78.7 us (0.950)
  Pallas kernels: 79.2 us -> 75.3 us
    pallas_call x1, Pallas kernels: 79.2 us -> 75.3 us  [fused(): pl.pallas_call(functools.partial(fused_kernel, n_seq, n_dp, group), out_s...]
where the time goes in v3:
time: 78.7 us; the launch traced here: 78.2 us
  Pallas kernels  75.3 us (96%)
  local copies, waits for them, and re-layouts  2.24 us (3%)
    pallas_call x1, Pallas kernels, fused(): pl.pallas_call(functools.partial(fused_kernel, n_seq, n_dp, group), out_s...  75.3 us
    broadcast_in_dim x1, local copies, waits for them, and re-layouts, fused(): return blocks.transpose(1, 0, 2)[None]  2.24 us

profile of v3, /device:TPU:25, one launch (start us, length us, event | category | flops | bytes accessed | tf_op | source)
XLA Modules:
  0.0 78.2 jit_solution(14334279142885136903)
XLA Ops:
  0.7 75.3 %shard_map.91 = bf16[4,64,1024]{2,1,0:T(8,128)(2,1)} custom-call(bf16[1,64,4096]{2,1,0:T(8,128)(2,1)} %q_ref.1, bf16[1,64,512]{2,1,0:T(8,128)(2,1)} %nk_ref.1, bf16[1,64,512]{2,1,0:T(8,128)(2,1)} %nv_ref.1, bf16[1,512,512]{2,1,0:T(8,128)(2,1)} %ck_ref.1, bf16[1,512,512]{2,1,0:T(8,128)(2,1)} %cv_ref.1, s32[1,1]{1,0:T(1,128)S(6)} %copy.11.keep_ref, ...), custom_call_target="tpu_custom_call" | custom-call | tf_op jit(solution)/shard_map/pallas_call | solution.py:491
  75.9 2.2 %copy.10 = bf16[1,64,4,1024]{3,2,1,0:T(4,128)(2,1)} copy(bf16[1,64,4,1024]{3,1,2,0:T(8,128)(2,1)} %bitcast.3) | data formatting | bytes 1048576 | tf_op jit(solution)/shard_map/broadcast_in_dim | solution.py:530
